TPU v7x, 512 devices: a whole 4x8x8 slice. The times are simulated.
512 devices in a mesh: tok: 16 (over y, core), voc: 32 (over x, z).
Axes of the slice: x: 4, y: 8, z: 8, core: 2. Of those that a mesh axis runs over, the one named last changes fastest.
Arguments:
- hidden: bfloat16 [4096, 2048], P('tok')
- panel: bfloat16 [2048, 8192], P(None, 'voc'), may hold values from -0.25 to 0.25
- in_proj: bfloat16 [2048, 64], replicated, may hold values from -0.125 to 0.125
- out_proj: bfloat16 [8192, 64], P('voc'), may hold values from -6 to 6
- targets: int32 [4096], P('tok'), may hold values from 0 to 8191
- keep: int32 [4096], P('tok'), may hold values 0 or 1
- span_ids: int32 [4096], P('tok'), may hold values from 0 to 511, as said below
- store: bfloat16 [131072, 4096], P(('tok', 'voc')), may hold values from -6 to 6
Outputs:
- hidden_grad: bfloat16 [4096, 2048], P('tok', 'voc')
- scores: float32 [512, 131072], P(None, ('tok', 'voc'))
Inputs may be any that keep to these rules, and one draw needn't show every extreme that they name: `span_ids`: tokens k * 256 to (k + 1) * 256 - 1 hold exactly the spans k * 32 to (k + 1) * 32 - 1 in increasing order, each of one or more tokens.
All inputs are finite; a program needn't handle non-finite values. No bound on the sum of `keep` on one device may be relied on, other than what follows from the above.
Results may differ from a plain program's by a relative error of at most 0.018.
Values may be sent and summed in bfloat16 or wider, within the bound.
No kernel may reach another device: no remote copies, remote signals or barrier semaphores. Data moves between devices by JAX's collectives and lax.ppermute only.
A program may use at most 64 MiB of HBM per device.

v0:
```python
import jax
import jax.numpy as jnp
from jax import lax
from jax.sharding import PartitionSpec as P

RANK = 64
SPAN_DEV = 32


def sent_to_all(array, axis):
    devices = lax.axis_size(axis)
    return lax.all_to_all(
        jnp.broadcast_to(array[None], (devices, *array.shape)), axis, 0, 0, tiled=True
    )


def collected_together(array, axis):
    leaves = jax.tree.leaves(array)
    order = sorted(range(len(leaves)), key=lambda k: -leaves[k].size)
    width = (1, *leaves[order[0]].shape)[-1]
    lines = [
        jnp.pad(leaves[k].reshape(-1), (0, -leaves[k].size % width)).reshape(-1, width)
        for k in order
    ]
    both, at, found = (sent_to_all(jnp.concatenate(lines), axis), 0, {})
    for k, line in zip(order, lines):
        share = both[:, at : at + len(line)].reshape(len(both), -1)
        found[k] = share[:, : leaves[k].size].reshape(-1, *leaves[k].shape)
        at += len(line)
    numbers = iter(range(len(leaves)))
    return jax.tree.map(lambda _: found[next(numbers)], array)


def combined_pairwise(pieces, combine):
    while len(jax.tree.leaves(pieces)[0]) > 1:
        pieces = jax.vmap(combine)(
            *(jax.tree.map(lambda part: part[side::2], pieces) for side in (0, 1))
        )
    return jax.tree.map(lambda part: part[0], pieces)


def merged(array, axis, combine):
    pieces = collected_together(array, axis)
    return combined_pairwise(pieces, combine)


def in_blocks(array, dim, devices):
    lengths = array.shape
    parts = array.reshape(*lengths[:dim], devices, lengths[dim] // devices, *lengths[dim + 1 :])
    return jnp.moveaxis(parts, dim, 0)


def sum_at_owner(array, axis, dim):
    devices = lax.axis_size(axis)
    parts = lax.all_to_all(in_blocks(array, dim, devices), axis, 0, 0, tiled=True)
    return jnp.sum(parts.astype(jnp.float32), axis=0)


def of_everyone(array, axis):
    everything = sent_to_all(array, axis)
    return jnp.sum(everything.astype(jnp.float32), axis=0)


def combine_stats(first, second):
    top = jnp.maximum(first[0], second[0])
    total = first[1] * jnp.exp(first[0] - top) + second[1] * jnp.exp(second[0] - top)
    return (top, total)


def span_sums(member, inner, outer):
    weighted = member[:, :, None] * inner[None, :, :]
    summed = lax.dot_general(
        weighted,
        outer,
        (((1,), (0,)), ((), ())),
        precision=lax.Precision.HIGHEST,
        preferred_element_type=jnp.float32,
    )
    return summed.reshape(member.shape[0], inner.shape[1] * outer.shape[1])


def body(hidden, panel, in_proj, out_proj, targets, keep, span_ids, store):
    panel_cols = panel.shape[1]
    logits = jnp.dot(hidden, panel, preferred_element_type=jnp.float32)
    local_top = jnp.max(logits, axis=1)
    local_total = jnp.sum(jnp.exp(logits - local_top[:, None]), axis=1)
    top, total = merged((local_top, local_total), "voc", combine_stats)
    lse = top + jnp.log(total)
    columns = lax.axis_index("voc") * panel_cols + jnp.arange(panel_cols, dtype=jnp.int32)
    onehot = (targets[:, None] == columns[None, :]).astype(jnp.float32)
    grad = ((jnp.exp(logits - lse[:, None]) - onehot) * keep.astype(jnp.float32)[:, None]).astype(
        jnp.bfloat16
    )
    partial_hidden = lax.dot_general(
        grad, panel, (((1,), (1,)), ((), ())), preferred_element_type=jnp.float32
    )
    hidden_grad = sum_at_owner(partial_hidden.astype(jnp.bfloat16), "voc", 1).astype(jnp.bfloat16)
    inner = jnp.dot(hidden, in_proj, preferred_element_type=jnp.float32)
    outer_part = jnp.dot(grad, out_proj, preferred_element_type=jnp.float32)
    local_span = span_ids - lax.axis_index("tok") * SPAN_DEV
    member = (local_span[None, :] == jnp.arange(SPAN_DEV, dtype=jnp.int32)[:, None]).astype(
        jnp.float32
    )
    outer = of_everyone(outer_part.astype(jnp.bfloat16), "voc").astype(jnp.float32)
    queries = span_sums(member, inner, outer).astype(jnp.bfloat16)
    scores = (
        lax.dot_general(
            lax.all_gather(queries, "tok", axis=0, tiled=True),
            store,
            (((1,), (1,)), ((), ())),
            preferred_element_type=jnp.float32,
        )
        / RANK
    )
    return (hidden_grad, scores)


def solution(mesh):
    placed = (
        P("tok", None),
        P(None, "voc"),
        P(),
        P("voc", None),
        P("tok"),
        P("tok"),
        P("tok"),
        P(("tok", "voc"), None),
    )
    return jax.shard_map(
        body,
        mesh=mesh,
        in_specs=placed,
        out_specs=(P("tok", "voc"), P(None, ("tok", "voc"))),
        check_vma=False,
    )
```

profile of v0, /device:TPU:1, one launch (start us, length us, event | category | flops | bytes accessed | tf_op | source)
XLA Modules:
  0.0 127.9 jit_solution(8398585282720557890)
XLA Ops:
  7.2 0.0 copy-start
  7.2 0.0 copy-start.4
  7.2 0.0 copy-start.3
  7.2 2.2 %fusion.12 = (f32[256]{0:T(256)S(1)}, f32[256,256]{0,1:T(8,128)S(1)}) fusion(bf16[256,2048]{1,0:T(8,128)(2,1)} %param.8, bf16[2048,256]{1,0:T(8,128)(2,1)} %param.9), kind=kOutput, calls=%fused_computation.30 | convolution fusion | flops 268500736 | bytes 2360320 | tf_op jit(solution)/shard_map/dot_general | solution.py:84
  9.4 0.1 exponential_reduce_fusion
  9.5 0.7 broadcast_in_dim.4
  10.2 13.7 %all-to-all-start = ((f32[32,2,256]{2,1,0:T(2,128)}), f32[32,2,256]{2,1,0:T(2,128)S(1)}, u32[]{:S(2)}, u32[]{:S(2)}) async-start(f32[32,2,256]{2,1,0:T(2,128)} %broadcast_in_dim.4), calls=%async_computation | async-start | bytes 131072 | tf_op jit(solution)/shard_map/all_to_all | solution.py:12
  23.9 0.0 copy-done.4
  23.9 8.8 %all-to-all-done = f32[32,2,256]{2,1,0:T(2,128)S(1)} async-done(((f32[32,2,256]{2,1,0:T(2,128)}), f32[32,2,256]{2,1,0:T(2,128)S(1)}, u32[]{:S(2)}, u32[]{:S(2)}) %all-to-all-start) | async-done | bytes 65568 | tf_op jit(solution)/shard_map/all_to_all | solution.py:12
  32.7 0.1 fusion.11
  32.8 0.0 copy-start.5
  32.8 0.0 copy-start.1
  33.2 0.0 copy-done.3
  33.3 1.0 convolution_convert_fusion.1
  34.2 1.2 broadcast_in_dim.5
  35.4 4.7 %all-to-all-start.2 = ((bf16[32,256,64]{1,2,0:T(8,128)(2,1)}), bf16[32,256,64]{1,2,0:T(8,128)(2,1)}, u32[]{:S(2)}, u32[]{:S(2)}) async-start(bf16[32,256,64]{1,2,0:T(8,128)(2,1)} %broadcast_in_dim.5), calls=%async_computation.2 | async-start | bytes 2097152 | tf_op jit(solution)/shard_map/all_to_all | solution.py:12
  40.1 0.0 all-gather.2.cloned.1.call-start
  40.1 0.0 copy-done.5
  40.2 0.0 copy-done.1
  40.2 1.4 %fusion.13 = f32[256,64]{0,1:T(8,128)S(1)} fusion(bf16[256,2048]{1,0:T(8,128)(2,1)S(1)} %copy-done.1, bf16[2048,64]{0,1:T(8,128)(2,1)} %param.10), kind=kOutput, calls=%fused_computation.31 | convolution fusion | flops 67108864 | bytes 1376256 | tf_op jit(solution)/shard_map/dot_general | solution.py:98
  41.6 0.0 copy-start.2
  41.6 22.9 %all-to-all-done.2 = bf16[32,256,64]{1,2,0:T(8,128)(2,1)} async-done(((bf16[32,256,64]{1,2,0:T(8,128)(2,1)}), bf16[32,256,64]{1,2,0:T(8,128)(2,1)}, u32[]{:S(2)}, u32[]{:S(2)}) %all-to-all-start.2) | async-done | bytes 1048608 | tf_op jit(solution)/shard_map/all_to_all | solution.py:12
  64.5 1.4 %convert_reduce_fusion = f32[256,64]{0,1:T(8,128)S(1)} fusion(bf16[32,256,64]{1,2,0:T(8,128)(2,1)} %all-to-all-done.2), kind=kLoop, calls=%fused_computation.1 | loop fusion | flops 1032192 | bytes 1114112 | tf_op jit(solution)/shard_map/reduce_sum | solution.py:61
  65.9 2.6 %fusion.2 = bf16[32,64,64]{2,1,0:T(8,128)(2,1)} fusion(f32[256,64]{0,1:T(8,128)S(1)} %fusion.13, f32[32,256]{1,0:T(8,128)S(1)} %fusion.8, f32[256,64]{0,1:T(8,128)S(1)} %convert_reduce_fusion), kind=kOutput, calls=%fused_computation.4 | convolution fusion | flops 403308544 | bytes 425984 | tf_op jit(solution)/shard_map/dot_general | solution.py:72
  68.5 2.2 %convert_element_type.41 = bf16[32,4096]{1,0:T(8,128)(2,1)} reshape(bf16[32,64,64]{2,1,0:T(8,128)(2,1)} %fusion.2) | data formatting | bytes 524288 | tf_op jit(solution)/shard_map/convert_element_type | solution.py:105
  70.7 0.0 all-gather.2.cloned.1.call-update
  70.7 0.0 copy-done.2
  70.7 1.5 %convolution_convert_fusion = bf16[256,2048]{1,0:T(8,128)(2,1)} fusion(bf16[2048,256]{1,0:T(8,128)(2,1)S(1)} %copy-done.2, f32[256,256]{0,1:T(8,128)S(1)} %get-tuple-element.13, f32[256]{0:T(256)S(1)} %convert_element_type.34, s32[256]{0:T(256)S(1)} %copy-done.3, f32[256]{0:T(256)S(1)} %bitcast.24, s32[256]{0:T(256)S(1)} %iota_add_fusion), kind=kOutput, calls=%fused_computation | convolution fusion | flops 269352960 | bytes 2363392 | tf_op jit(solution)/shard_map/dot_general | solution.py:94
  72.3 2.3 %copy.14 = bf16[256,2048]{0,1:T(8,128)(2,1)} copy(bf16[256,2048]{1,0:T(8,128)(2,1)} %convolution_convert_fusion) | data formatting | bytes 2097152 | tf_op jit(solution)/shard_map/convert_element_type | solution.py:97
  74.5 32.7 %all_to_all.15 = bf16[32,256,64]{1,2,0:T(8,128)(2,1)S(1)} all-to-all(bf16[32,256,64]{1,2,0:T(8,128)(2,1)} %bitcast.21), channel_id=1, replica_groups=mesh['tok'=16,'voc'=32] {'voc'}, dimensions={0} | all-to-all | bytes 2097152 | tf_op jit(solution)/shard_map/all_to_all | solution.py:55
  107.2 0.8 reduce_sum.31
  108.0 8.8 %all-gather.2.cloned.1.call-done = bf16[512,4096]{1,0:T(8,128)(2,1)} async-done(((bf16[32,4096]{1,0:T(8,128)(2,1)}), bf16[512,4096]{1,0:T(8,128)(2,1)}) %all-gather.2.cloned.1.call-update) | async-done | bytes 4194320 | tf_op jit(solution)/shard_map/all_gather | solution.py:108
  116.8 0.0 copy-done
  116.8 4.3 %convolution_multiply_fusion = f32[512,256]{1,0:T(8,128)} fusion(bf16[512,4096]{1,0:T(8,128)(2,1)} %all-gather.2.cloned.1.call-done, bf16[256,4096]{1,0:T(8,128)(2,1)S(1)} %copy-done), kind=kOutput, calls=%fused_computation.5 | convolution fusion | flops 1073872896 | bytes 6815744 | tf_op jit(solution)/shard_map/dot_general | solution.py:107
  (27 shorter events, 0.4 us)
Async XLA Ops:
  7.2 109.6 %copy-start = (bf16[256,4096]{1,0:T(8,128)(2,1)S(1)}, bf16[256,4096]{1,0:T(8,128)(2,1)}, u32[]{:S(2)}) copy-start(bf16[256,4096]{1,0:T(8,128)(2,1)} %param.15) | copy-start | bytes 6291460
  7.2 16.7 %copy-start.4 = (s32[256]{0:T(256)S(1)}, s32[256]{0:T(256)}, u32[]{:S(2)}) copy-start(s32[256]{0:T(256)} %param.13) | copy-start | bytes 3076
  7.2 26.1 %copy-start.3 = (s32[256]{0:T(256)S(1)}, s32[256]{0:T(256)}, u32[]{:S(2)}) copy-start(s32[256]{0:T(256)} %param.12) | copy-start | bytes 3076
  10.2 22.6 %all-to-all-start = ((f32[32,2,256]{2,1,0:T(2,128)}), f32[32,2,256]{2,1,0:T(2,128)S(1)}, u32[]{:S(2)}, u32[]{:S(2)}) async-start(f32[32,2,256]{2,1,0:T(2,128)} %broadcast_in_dim.4), calls=%async_computation | async-start | bytes 131072 | tf_op jit(solution)/shard_map/all_to_all | solution.py:12
  32.8 7.3 %copy-start.5 = (s32[256]{0:T(256)S(1)}, s32[256]{0:T(256)}, u32[]{:S(2)}) copy-start(s32[256]{0:T(256)} %param.14) | copy-start | bytes 3076
  32.8 7.4 %copy-start.1 = (bf16[256,2048]{1,0:T(8,128)(2,1)S(1)}, bf16[256,2048]{1,0:T(8,128)(2,1)}, u32[]{:S(2)}) copy-start(bf16[256,2048]{1,0:T(8,128)(2,1)} %param.8) | copy-start | bytes 3145732
  35.4 29.1 %all-to-all-start.2 = ((bf16[32,256,64]{1,2,0:T(8,128)(2,1)}), bf16[32,256,64]{1,2,0:T(8,128)(2,1)}, u32[]{:S(2)}, u32[]{:S(2)}) async-start(bf16[32,256,64]{1,2,0:T(8,128)(2,1)} %broadcast_in_dim.5), calls=%async_computation.2 | async-start | bytes 2097152 | tf_op jit(solution)/shard_map/all_to_all | solution.py:12
  40.1 76.7 %all-gather.2.cloned.1.call-start = ((), (), s32[]{:S(2)}) async-start(), calls=%async_computation.3 | async-start | bytes 4456448 | tf_op jit(solution)/shard_map/all_gather | solution.py:108
  41.6 29.1 %copy-start.2 = (bf16[2048,256]{1,0:T(8,128)(2,1)S(1)}, bf16[2048,256]{1,0:T(8,128)(2,1)}, u32[]{:S(2)}) copy-start(bf16[2048,256]{1,0:T(8,128)(2,1)} %param.9) | copy-start | bytes 3145732
Sparse Core Ops, SparseCore 0:
  70.8 45.9 all-gather.1
where the time goes:
time: 128 us
  waiting for transfers between devices  40.6 us (32%)
  blocking collectives  32.7 us (26%)
  starting transfers between devices  18.4 us (14%)
  between operations  14.2 us (11%)
  matrix products  13 us (10%)
  local copies, waits for them, and re-layouts  6.66 us (5%)
  other arithmetic  2.33 us (2%)
    all_to_all x1, blocking collectives, sum_at_owner(): lax.all_to_all(in_blocks(array, dim, devices), axis, 0, 0, tiled=True)  32.7 us
    all_to_all x2, waiting for transfers between devices, sent_to_all(): lax.all_to_all(jnp.broadcast_to(array[None], (devices, *array.shape)), ax...  31.8 us
    all_to_all x2, starting transfers between devices, sent_to_all(): lax.all_to_all(jnp.broadcast_to(array[None], (devices, *array.shape)), ax...  18.4 us
    all_gather x1, waiting for transfers between devices, body(): lax.all_gather(queries, 'tok', axis=0, tiled=True)  8.82 us
    dot_general x1, matrix products, body(): lax.dot_general(lax.all_gather(queries, 'tok', axis=0, tiled=True), store...  4.26 us
    dot_general x1, matrix products, span_sums(): lax.dot_general(weighted, outer, (((1,), (0,)), ((), ())), precision=lax....  2.58 us
  transfers between devices with their start and end apart: 3, of which 3 were waited for; matrix products, arithmetic and copies ran while one was open for 5% of the time, Pallas kernels for 0%

commit v1 on v0

--- a/solution.py
+++ b/solution.py
@@ -5,6 +5,24 @@
 
 RANK = 64
 SPAN_DEV = 32
+
+
+def ring_gather(value, axis, dim):
+    ways, here, step = (lax.axis_size(axis), lax.axis_index(axis), value.shape[dim])
+    dims = [n * ways if d == dim else n for d, n in enumerate(value.shape)]
+    full = lax.dynamic_update_slice_in_dim(
+        jnp.zeros(dims, value.dtype), value, here * step, axis=dim
+    )
+    going_up = going_down = value
+    for far in range(1, ways // 2 + 1):
+        going_up = lax.ppermute(going_up, axis, [(d, (d + 1) % ways) for d in range(ways)])
+        full = lax.dynamic_update_slice_in_dim(full, going_up, (here - far) % ways * step, axis=dim)
+        if 2 * far < ways:
+            going_down = lax.ppermute(going_down, axis, [(d, (d - 1) % ways) for d in range(ways)])
+            full = lax.dynamic_update_slice_in_dim(
+                full, going_down, (here + far) % ways * step, axis=dim
+            )
+    return full
 
 
 def sent_to_all(array, axis):
@@ -105,7 +123,7 @@
     queries = span_sums(member, inner, outer).astype(jnp.bfloat16)
     scores = (
         lax.dot_general(
-            lax.all_gather(queries, "tok", axis=0, tiled=True),
+            ring_gather(queries, "tok", 0),
             store,
             (((1,), (1,)), ((), ())),
             preferred_element_type=jnp.float32,

time: 128 us -> 149 us (1.16)
  the two profiles are of different devices: /device:TPU:1 before, /device:TPU:32 now
where the time goes in v1:
time: 149 us; the launch traced here: 148 us
  waiting for transfers between devices  84 us (56%)
  starting transfers between devices  43.8 us (29%)
  matrix products  9.08 us (6%)
  local copies, waits for them, and re-layouts  5.86 us (4%)
  other arithmetic  4.26 us (3%)
    all_to_all x2, waiting for transfers between devices, sent_to_all(): lax.all_to_all(jnp.broadcast_to(array[None], (devices, *array.shape)), ax...  32.9 us
    ppermute x8, waiting for transfers between devices, ring_gather(): lax.ppermute(going_up, axis, [(d, (d + 1) % ways) for d in range(ways)])  30.9 us
    ppermute x7, starting transfers between devices, ring_gather(): lax.ppermute(going_down, axis, [(d, (d - 1) % ways) for d in range(ways)])  20.7 us
    all_to_all x1, waiting for transfers between devices, sum_at_owner(): lax.all_to_all(in_blocks(array, dim, devices), axis, 0, 0, tiled=True)  20.2 us
    all_to_all x2, starting transfers between devices, sent_to_all(): lax.all_to_all(jnp.broadcast_to(array[None], (devices, *array.shape)), ax...  18 us
    all_to_all x1, starting transfers between devices, sum_at_owner(): lax.all_to_all(in_blocks(array, dim, devices), axis, 0, 0, tiled=True)  5.15 us
  transfers between devices with their start and end apart: 18, of which 10 were waited for; matrix products, arithmetic and copies ran while one was open for 8% of the time, Pallas kernels for 0%

profile of v1, /device:TPU:32, one launch (start us, length us, event | category | flops | bytes accessed | tf_op | source)
XLA Modules:
  0.0 148.2 jit_solution(12002320994797001017)
XLA Ops:
  0.6 0.0 copy-start
  0.7 0.0 copy-start.4
  0.7 2.2 %fusion.12 = (f32[256]{0:T(256)S(1)}, f32[256,256]{0,1:T(8,128)S(1)}) fusion(bf16[256,2048]{1,0:T(8,128)(2,1)} %param.8, bf16[2048,256]{1,0:T(8,128)(2,1)} %param.9), kind=kOutput, calls=%fused_computation.46 | convolution fusion | flops 268500736 | bytes 2360320 | tf_op jit(solution)/shard_map/dot_general | solution.py:102
  2.9 0.1 exponential_reduce_fusion
  3.0 0.7 broadcast_in_dim.6
  3.6 13.2 %all-to-all-start = ((f32[32,2,256]{2,1,0:T(2,128)}), f32[32,2,256]{2,1,0:T(2,128)S(1)}, u32[]{:S(2)}, u32[]{:S(2)}) async-start(f32[32,2,256]{2,1,0:T(2,128)} %broadcast_in_dim.6), calls=%async_computation | async-start | bytes 131072 | tf_op jit(solution)/shard_map/all_to_all | solution.py:30
  16.8 0.7 convert_element_type.34
  17.5 9.3 %all-to-all-done = f32[32,2,256]{2,1,0:T(2,128)S(1)} async-done(((f32[32,2,256]{2,1,0:T(2,128)}), f32[32,2,256]{2,1,0:T(2,128)S(1)}, u32[]{:S(2)}, u32[]{:S(2)}) %all-to-all-start) | async-done | bytes 65568 | tf_op jit(solution)/shard_map/all_to_all | solution.py:30
  26.8 0.1 fusion.11
  27.3 1.0 convolution_convert_fusion.1
  28.3 1.1 broadcast_in_dim.8
  29.4 4.8 %all-to-all-start.2 = ((bf16[32,256,64]{1,2,0:T(8,128)(2,1)}), bf16[32,256,64]{1,2,0:T(8,128)(2,1)}, u32[]{:S(2)}, u32[]{:S(2)}) async-start(bf16[32,256,64]{1,2,0:T(8,128)(2,1)} %broadcast_in_dim.8), calls=%async_computation.2 | async-start | bytes 2097152 | tf_op jit(solution)/shard_map/all_to_all | solution.py:30
  34.2 1.6 %convolution_convert_fusion = bf16[256,2048]{1,0:T(8,128)(2,1)} fusion(bf16[2048,256]{1,0:T(8,128)(2,1)S(1)} %copy-done.1, f32[256,256]{0,1:T(8,128)S(1)} %get-tuple-element.13, f32[256]{0:T(256)S(1)} %convert_element_type.34, s32[256]{0:T(256)S(1)} %copy-done.4, f32[256]{0:T(256)S(1)} %bitcast.24, s32[256]{0:T(256)S(1)} %iota_add_fusion), kind=kOutput, calls=%fused_computation | convolution fusion | flops 269352960 | bytes 2363392 | tf_op jit(solution)/shard_map/dot_general | solution.py:112
  35.8 2.4 %copy.14 = bf16[256,2048]{0,1:T(8,128)(2,1)} copy(bf16[256,2048]{1,0:T(8,128)(2,1)} %convolution_convert_fusion) | data formatting | bytes 2097152 | tf_op jit(solution)/shard_map/convert_element_type | solution.py:115
  38.2 23.6 %all-to-all-done.2 = bf16[32,256,64]{1,2,0:T(8,128)(2,1)} async-done(((bf16[32,256,64]{1,2,0:T(8,128)(2,1)}), bf16[32,256,64]{1,2,0:T(8,128)(2,1)}, u32[]{:S(2)}, u32[]{:S(2)}) %all-to-all-start.2) | async-done | bytes 1048608 | tf_op jit(solution)/shard_map/all_to_all | solution.py:30
  61.7 5.1 %all-to-all-start.1 = ((bf16[32,256,64]{1,2,0:T(8,128)(2,1)}), bf16[32,256,64]{1,2,0:T(8,128)(2,1)}, u32[]{:S(2)}, u32[]{:S(2)}) async-start(bf16[32,256,64]{1,2,0:T(8,128)(2,1)} %bitcast.21), calls=%async_computation.1 | async-start | bytes 2097152 | tf_op jit(solution)/shard_map/all_to_all | solution.py:73
  67.3 0.4 fusion.13
  67.7 1.4 convert_reduce_fusion
  69.1 1.8 %fusion.2 = bf16[32,64,64]{2,1,0:T(8,128)(2,1)S(1)} fusion(f32[256,64]{0,1:T(8,128)S(1)} %fusion.13, f32[32,256]{1,0:T(8,128)S(1)} %fusion.8, f32[256,64]{0,1:T(8,128)S(1)} %convert_reduce_fusion), kind=kOutput, calls=%fused_computation.4 | convolution fusion | flops 403308544 | bytes 425984 | tf_op jit(solution)/shard_map/dot_general | solution.py:90
  70.9 0.5 convert_element_type.41
  71.3 0.0 collective-permute-start
  71.4 2.9 %collective-permute-start.1 = (bf16[32,4096]{1,0:T(8,128)(2,1)S(1)}, bf16[32,4096]{1,0:T(8,128)(2,1)S(1)}, u32[]{:S(2)}, u32[]{:S(2)}) collective-permute-start(bf16[32,4096]{1,0:T(8,128)(2,1)S(1)} %convert_element_type.41), channel_id=1, source_target_pairs={{0,480},{32,0},{64,32},{96,64},{128,96},{160,128},{192,160},{224,1... | collective-permute-start | bytes 786440 | tf_op jit(solution)/shard_map/ppermute | solution.py:21
  74.3 20.2 %all-to-all-done.1 = bf16[32,256,64]{1,2,0:T(8,128)(2,1)} async-done(((bf16[32,256,64]{1,2,0:T(8,128)(2,1)}), bf16[32,256,64]{1,2,0:T(8,128)(2,1)}, u32[]{:S(2)}, u32[]{:S(2)}) %all-to-all-start.1) | async-done | bytes 1048608 | tf_op jit(solution)/shard_map/all_to_all | solution.py:73
  94.5 2.0 %reduce_sum.31 = bf16[256,64]{0,1:T(8,128)(2,1)} reduce(bf16[32,256,64]{1,2,0:T(8,128)(2,1)} %all-to-all-done.1, bf16[]{:T(256)} %constant.102.clone.1), dimensions={0}, to_apply=%region_2.3 | reduce | flops 507904 | bytes 1081346 | tf_op jit(solution)/shard_map/reduce_sum | solution.py:74
  96.5 0.5 broadcast_in_dim.7
  97.0 0.0 collective-permute-start.2
  97.1 0.0 collective-permute-done.1
  97.1 2.9 %collective-permute-start.3 = (bf16[32,4096]{1,0:T(8,128)(2,1)S(1)}, bf16[32,4096]{1,0:T(8,128)(2,1)S(1)}, u32[]{:S(2)}, u32[]{:S(2)}) collective-permute-start(bf16[32,4096]{1,0:T(8,128)(2,1)S(1)} %collective-permute-done.1), channel_id=1, source_target_pairs={{0,480},{32,0},{64,32},{96,64},{128,96},{160,128},{192,160},{224,1... | collective-permute-start | bytes 786440 | tf_op jit(solution)/shard_map/ppermute | solution.py:21
  100.1 4.0 %collective-permute-done.2 = bf16[32,4096]{1,0:T(8,128)(2,1)S(1)} collective-permute-done((bf16[32,4096]{1,0:T(8,128)(2,1)S(1)}, bf16[32,4096]{1,0:T(8,128)(2,1)S(1)}, u32[]{:S(2)}, u32[]{:S(2)}) %collective-permute-start.2) | collective-permute-done | bytes 262176 | tf_op jit(solution)/shard_map/ppermute | solution.py:18
  104.1 0.0 collective-permute-start.4
  104.1 0.0 collective-permute-done.3
  104.1 3.0 %collective-permute-start.5 = (bf16[32,4096]{1,0:T(8,128)(2,1)S(1)}, bf16[32,4096]{1,0:T(8,128)(2,1)S(1)}, u32[]{:S(2)}, u32[]{:S(2)}) collective-permute-start(bf16[32,4096]{1,0:T(8,128)(2,1)S(1)} %collective-permute-done.3), channel_id=1, source_target_pairs={{0,480},{32,0},{64,32},{96,64},{128,96},{160,128},{192,160},{224,1... | collective-permute-start | bytes 786440 | tf_op jit(solution)/shard_map/ppermute | solution.py:21
  107.1 4.0 %collective-permute-done.4 = bf16[32,4096]{1,0:T(8,128)(2,1)S(1)} collective-permute-done((bf16[32,4096]{1,0:T(8,128)(2,1)S(1)}, bf16[32,4096]{1,0:T(8,128)(2,1)S(1)}, u32[]{:S(2)}, u32[]{:S(2)}) %collective-permute-start.4) | collective-permute-done | bytes 262176 | tf_op jit(solution)/shard_map/ppermute | solution.py:18
  111.1 0.0 collective-permute-start.6
  111.1 0.0 collective-permute-done.5
  111.1 3.0 %collective-permute-start.7 = (bf16[32,4096]{1,0:T(8,128)(2,1)S(1)}, bf16[32,4096]{1,0:T(8,128)(2,1)S(1)}, u32[]{:S(2)}, u32[]{:S(2)}) collective-permute-start(bf16[32,4096]{1,0:T(8,128)(2,1)S(1)} %collective-permute-done.5), channel_id=1, source_target_pairs={{0,480},{32,0},{64,32},{96,64},{128,96},{160,128},{192,160},{224,1... | collective-permute-start | bytes 786440 | tf_op jit(solution)/shard_map/ppermute | solution.py:21
  114.1 4.0 %collective-permute-done.6 = bf16[32,4096]{1,0:T(8,128)(2,1)S(1)} collective-permute-done((bf16[32,4096]{1,0:T(8,128)(2,1)S(1)}, bf16[32,4096]{1,0:T(8,128)(2,1)S(1)}, u32[]{:S(2)}, u32[]{:S(2)}) %collective-permute-start.6) | collective-permute-done | bytes 262176 | tf_op jit(solution)/shard_map/ppermute | solution.py:18
  118.1 0.0 collective-permute-start.8
  118.1 0.0 collective-permute-done.7
  118.1 3.0 %collective-permute-start.9 = (bf16[32,4096]{1,0:T(8,128)(2,1)S(1)}, bf16[32,4096]{1,0:T(8,128)(2,1)S(1)}, u32[]{:S(2)}, u32[]{:S(2)}) collective-permute-start(bf16[32,4096]{1,0:T(8,128)(2,1)S(1)} %collective-permute-done.7), channel_id=1, source_target_pairs={{0,480},{32,0},{64,32},{96,64},{128,96},{160,128},{192,160},{224,1... | collective-permute-start | bytes 786440 | tf_op jit(solution)/shard_map/ppermute | solution.py:21
  121.1 4.0 %collective-permute-done.8 = bf16[32,4096]{1,0:T(8,128)(2,1)S(1)} collective-permute-done((bf16[32,4096]{1,0:T(8,128)(2,1)S(1)}, bf16[32,4096]{1,0:T(8,128)(2,1)S(1)}, u32[]{:S(2)}, u32[]{:S(2)}) %collective-permute-start.8) | collective-permute-done | bytes 262176 | tf_op jit(solution)/shard_map/ppermute | solution.py:18
  125.1 0.0 collective-permute-start.10
  125.1 3.0 %collective-permute-start.11 = (bf16[32,4096]{1,0:T(8,128)(2,1)S(1)}, bf16[32,4096]{1,0:T(8,128)(2,1)S(1)}, u32[]{:S(2)}, u32[]{:S(2)}) collective-permute-start(bf16[32,4096]{1,0:T(8,128)(2,1)S(1)} %collective-permute-done.9), channel_id=1, source_target_pairs={{0,480},{32,0},{64,32},{96,64},{128,96},{160,128},{192,160},{224,1... | collective-permute-start | bytes 786440 | tf_op jit(solution)/shard_map/ppermute | solution.py:21
  128.1 4.0 %collective-permute-done.10 = bf16[32,4096]{1,0:T(8,128)(2,1)S(1)} collective-permute-done((bf16[32,4096]{1,0:T(8,128)(2,1)S(1)}, bf16[32,4096]{1,0:T(8,128)(2,1)S(1)}, u32[]{:S(2)}, u32[]{:S(2)}) %collective-permute-start.10) | collective-permute-done | bytes 262176 | tf_op jit(solution)/shard_map/ppermute | solution.py:18
  132.1 3.0 %collective-permute-start.13 = (bf16[32,4096]{1,0:T(8,128)(2,1)S(1)}, bf16[32,4096]{1,0:T(8,128)(2,1)S(1)}, u32[]{:S(2)}, u32[]{:S(2)}) collective-permute-start(bf16[32,4096]{1,0:T(8,128)(2,1)S(1)} %collective-permute-done.11), channel_id=1, source_target_pairs={{0,480},{32,0},{64,32},{96,64},{128,96},{160,128},{192,160},{224,1... | collective-permute-start | bytes 786440 | tf_op jit(solution)/shard_map/ppermute | solution.py:21
  135.1 4.0 %collective-permute-done.12 = bf16[32,4096]{1,0:T(8,128)(2,1)S(1)} collective-permute-done((bf16[32,4096]{1,0:T(8,128)(2,1)S(1)}, bf16[32,4096]{1,0:T(8,128)(2,1)S(1)}, u32[]{:S(2)}, u32[]{:S(2)}) %collective-permute-start.12) | collective-permute-done | bytes 262176 | tf_op jit(solution)/shard_map/ppermute | solution.py:18
  139.2 6.9 %collective-permute-done.14 = bf16[32,4096]{1,0:T(8,128)(2,1)S(1)} collective-permute-done((bf16[32,4096]{1,0:T(8,128)(2,1)S(1)}, bf16[32,4096]{1,0:T(8,128)(2,1)S(1)}, u32[]{:S(2)}, u32[]{:S(2)}) %collective-permute-start.14) | collective-permute-done | bytes 262176 | tf_op jit(solution)/shard_map/ppermute | solution.py:18
  146.2 2.1 %convolution_multiply_fusion = f32[512,256]{1,0:T(8,128)} fusion(bf16[512,4096]{1,0:T(8,128)(2,1)S(1)} %constant_dynamic-update-slice_fusion, bf16[256,4096]{1,0:T(8,128)(2,1)S(1)} %copy-done), kind=kOutput, calls=%fused_computation.5 | convolution fusion | flops 1073872896 | bytes 6815744 | tf_op jit(solution)/shard_map/dot_general | solution.py:125
  (58 shorter events, 0.8 us)
Async XLA Ops:
  0.6 145.5 %copy-start = (bf16[256,4096]{1,0:T(8,128)(2,1)S(1)}, bf16[256,4096]{1,0:T(8,128)(2,1)}, u32[]{:S(2)}) copy-start(bf16[256,4096]{1,0:T(8,128)(2,1)} %param.15) | copy-start | bytes 6291460
  0.6 33.6 %copy-start.1 = (bf16[2048,256]{1,0:T(8,128)(2,1)S(1)}, bf16[2048,256]{1,0:T(8,128)(2,1)}, u32[]{:S(2)}) copy-start(bf16[2048,256]{1,0:T(8,128)(2,1)} %param.9) | copy-start | bytes 3145732
  0.7 33.6 %copy-start.4 = (s32[256]{0:T(256)S(1)}, s32[256]{0:T(256)}, u32[]{:S(2)}) copy-start(s32[256]{0:T(256)} %param.12) | copy-start | bytes 3076
  3.6 23.2 %all-to-all-start = ((f32[32,2,256]{2,1,0:T(2,128)}), f32[32,2,256]{2,1,0:T(2,128)S(1)}, u32[]{:S(2)}, u32[]{:S(2)}) async-start(f32[32,2,256]{2,1,0:T(2,128)} %broadcast_in_dim.6), calls=%async_computation | async-start | bytes 131072 | tf_op jit(solution)/shard_map/all_to_all | solution.py:30
  29.4 37.8 %copy-start.5 = (s32[256]{0:T(256)S(1)}, s32[256]{0:T(256)}, u32[]{:S(2)}) copy-start(s32[256]{0:T(256)} %param.14) | copy-start | bytes 3076
  29.4 32.3 %all-to-all-start.2 = ((bf16[32,256,64]{1,2,0:T(8,128)(2,1)}), bf16[32,256,64]{1,2,0:T(8,128)(2,1)}, u32[]{:S(2)}, u32[]{:S(2)}) async-start(bf16[32,256,64]{1,2,0:T(8,128)(2,1)} %broadcast_in_dim.8), calls=%async_computation.2 | async-start | bytes 2097152 | tf_op jit(solution)/shard_map/all_to_all | solution.py:30
  35.8 31.4 %copy-start.2 = (bf16[256,2048]{1,0:T(8,128)(2,1)S(1)}, bf16[256,2048]{1,0:T(8,128)(2,1)}, u32[]{:S(2)}) copy-start(bf16[256,2048]{1,0:T(8,128)(2,1)} %param.8) | copy-start | bytes 3145732
  35.8 31.5 %copy-start.3 = (bf16[2048,64]{0,1:T(8,128)(2,1)S(1)}, bf16[2048,64]{0,1:T(8,128)(2,1)}, u32[]{:S(2)}) copy-start(bf16[2048,64]{0,1:T(8,128)(2,1)} %param.10) | copy-start | bytes 786436
  61.7 32.8 %all-to-all-start.1 = ((bf16[32,256,64]{1,2,0:T(8,128)(2,1)}), bf16[32,256,64]{1,2,0:T(8,128)(2,1)}, u32[]{:S(2)}, u32[]{:S(2)}) async-start(bf16[32,256,64]{1,2,0:T(8,128)(2,1)} %bitcast.21), calls=%async_computation.1 | async-start | bytes 2097152 | tf_op jit(solution)/shard_map/all_to_all | solution.py:73
  71.3 25.7 %collective-permute-start = (bf16[32,4096]{1,0:T(8,128)(2,1)S(1)}, bf16[32,4096]{1,0:T(8,128)(2,1)S(1)}, u32[]{:S(2)}, u32[]{:S(2)}) collective-permute-start(bf16[32,4096]{1,0:T(8,128)(2,1)S(1)} %convert_element_type.41), channel_id=1, source_target_pairs={{0,32},{32,64},{64,96},{96,128},{128,160},{160,192},{192,224},{224... | collective-permute-start | bytes 786440 | tf_op jit(solution)/shard_map/ppermute | solution.py:18
  71.4 25.7 %collective-permute-start.1 = (bf16[32,4096]{1,0:T(8,128)(2,1)S(1)}, bf16[32,4096]{1,0:T(8,128)(2,1)S(1)}, u32[]{:S(2)}, u32[]{:S(2)}) collective-permute-start(bf16[32,4096]{1,0:T(8,128)(2,1)S(1)} %convert_element_type.41), channel_id=1, source_target_pairs={{0,480},{32,0},{64,32},{96,64},{128,96},{160,128},{192,160},{224,1... | collective-permute-start | bytes 786440 | tf_op jit(solution)/shard_map/ppermute | solution.py:21
  97.0 7.0 %collective-permute-start.2 = (bf16[32,4096]{1,0:T(8,128)(2,1)S(1)}, bf16[32,4096]{1,0:T(8,128)(2,1)S(1)}, u32[]{:S(2)}, u32[]{:S(2)}) collective-permute-start(bf16[32,4096]{1,0:T(8,128)(2,1)S(1)} %collective-permute-done), channel_id=1, source_target_pairs={{0,32},{32,64},{64,96},{96,128},{128,160},{160,192},{192,224},{224... | collective-permute-start | bytes 786440 | tf_op jit(solution)/shard_map/ppermute | solution.py:18
  97.1 7.0 %collective-permute-start.3 = (bf16[32,4096]{1,0:T(8,128)(2,1)S(1)}, bf16[32,4096]{1,0:T(8,128)(2,1)S(1)}, u32[]{:S(2)}, u32[]{:S(2)}) collective-permute-start(bf16[32,4096]{1,0:T(8,128)(2,1)S(1)} %collective-permute-done.1), channel_id=1, source_target_pairs={{0,480},{32,0},{64,32},{96,64},{128,96},{160,128},{192,160},{224,1... | collective-permute-start | bytes 786440 | tf_op jit(solution)/shard_map/ppermute | solution.py:21
  104.1 7.0 %collective-permute-start.4 = (bf16[32,4096]{1,0:T(8,128)(2,1)S(1)}, bf16[32,4096]{1,0:T(8,128)(2,1)S(1)}, u32[]{:S(2)}, u32[]{:S(2)}) collective-permute-start(bf16[32,4096]{1,0:T(8,128)(2,1)S(1)} %collective-permute-done.2), channel_id=1, source_target_pairs={{0,32},{32,64},{64,96},{96,128},{128,160},{160,192},{192,224},{224... | collective-permute-start | bytes 786440 | tf_op jit(solution)/shard_map/ppermute | solution.py:18
  104.1 7.0 %collective-permute-start.5 = (bf16[32,4096]{1,0:T(8,128)(2,1)S(1)}, bf16[32,4096]{1,0:T(8,128)(2,1)S(1)}, u32[]{:S(2)}, u32[]{:S(2)}) collective-permute-start(bf16[32,4096]{1,0:T(8,128)(2,1)S(1)} %collective-permute-done.3), channel_id=1, source_target_pairs={{0,480},{32,0},{64,32},{96,64},{128,96},{160,128},{192,160},{224,1... | collective-permute-start | bytes 786440 | tf_op jit(solution)/shard_map/ppermute | solution.py:21
  111.1 7.0 %collective-permute-start.6 = (bf16[32,4096]{1,0:T(8,128)(2,1)S(1)}, bf16[32,4096]{1,0:T(8,128)(2,1)S(1)}, u32[]{:S(2)}, u32[]{:S(2)}) collective-permute-start(bf16[32,4096]{1,0:T(8,128)(2,1)S(1)} %collective-permute-done.4), channel_id=1, source_target_pairs={{0,32},{32,64},{64,96},{96,128},{128,160},{160,192},{192,224},{224... | collective-permute-start | bytes 786440 | tf_op jit(solution)/shard_map/ppermute | solution.py:18
  111.1 7.0 %collective-permute-start.7 = (bf16[32,4096]{1,0:T(8,128)(2,1)S(1)}, bf16[32,4096]{1,0:T(8,128)(2,1)S(1)}, u32[]{:S(2)}, u32[]{:S(2)}) collective-permute-start(bf16[32,4096]{1,0:T(8,128)(2,1)S(1)} %collective-permute-done.5), channel_id=1, source_target_pairs={{0,480},{32,0},{64,32},{96,64},{128,96},{160,128},{192,160},{224,1... | collective-permute-start | bytes 786440 | tf_op jit(solution)/shard_map/ppermute | solution.py:21
  118.1 7.0 %collective-permute-start.8 = (bf16[32,4096]{1,0:T(8,128)(2,1)S(1)}, bf16[32,4096]{1,0:T(8,128)(2,1)S(1)}, u32[]{:S(2)}, u32[]{:S(2)}) collective-permute-start(bf16[32,4096]{1,0:T(8,128)(2,1)S(1)} %collective-permute-done.6), channel_id=1, source_target_pairs={{0,32},{32,64},{64,96},{96,128},{128,160},{160,192},{192,224},{224... | collective-permute-start | bytes 786440 | tf_op jit(solution)/shard_map/ppermute | solution.py:18
  118.1 7.0 %collective-permute-start.9 = (bf16[32,4096]{1,0:T(8,128)(2,1)S(1)}, bf16[32,4096]{1,0:T(8,128)(2,1)S(1)}, u32[]{:S(2)}, u32[]{:S(2)}) collective-permute-start(bf16[32,4096]{1,0:T(8,128)(2,1)S(1)} %collective-permute-done.7), channel_id=1, source_target_pairs={{0,480},{32,0},{64,32},{96,64},{128,96},{160,128},{192,160},{224,1... | collective-permute-start | bytes 786440 | tf_op jit(solution)/shard_map/ppermute | solution.py:21
  125.1 7.0 %collective-permute-start.10 = (bf16[32,4096]{1,0:T(8,128)(2,1)S(1)}, bf16[32,4096]{1,0:T(8,128)(2,1)S(1)}, u32[]{:S(2)}, u32[]{:S(2)}) collective-permute-start(bf16[32,4096]{1,0:T(8,128)(2,1)S(1)} %collective-permute-done.8), channel_id=1, source_target_pairs={{0,32},{32,64},{64,96},{96,128},{128,160},{160,192},{192,224},{224... | collective-permute-start | bytes 786440 | tf_op jit(solution)/shard_map/ppermute | solution.py:18
  125.1 7.0 %collective-permute-start.11 = (bf16[32,4096]{1,0:T(8,128)(2,1)S(1)}, bf16[32,4096]{1,0:T(8,128)(2,1)S(1)}, u32[]{:S(2)}, u32[]{:S(2)}) collective-permute-start(bf16[32,4096]{1,0:T(8,128)(2,1)S(1)} %collective-permute-done.9), channel_id=1, source_target_pairs={{0,480},{32,0},{64,32},{96,64},{128,96},{160,128},{192,160},{224,1... | collective-permute-start | bytes 786440 | tf_op jit(solution)/shard_map/ppermute | solution.py:21
  132.1 7.0 %collective-permute-start.12 = (bf16[32,4096]{1,0:T(8,128)(2,1)S(1)}, bf16[32,4096]{1,0:T(8,128)(2,1)S(1)}, u32[]{:S(2)}, u32[]{:S(2)}) collective-permute-start(bf16[32,4096]{1,0:T(8,128)(2,1)S(1)} %collective-permute-done.10), channel_id=1, source_target_pairs={{0,32},{32,64},{64,96},{96,128},{128,160},{160,192},{192,224},{224... | collective-permute-start | bytes 786440 | tf_op jit(solution)/shard_map/ppermute | solution.py:18
  132.1 7.0 %collective-permute-start.13 = (bf16[32,4096]{1,0:T(8,128)(2,1)S(1)}, bf16[32,4096]{1,0:T(8,128)(2,1)S(1)}, u32[]{:S(2)}, u32[]{:S(2)}) collective-permute-start(bf16[32,4096]{1,0:T(8,128)(2,1)S(1)} %collective-permute-done.11), channel_id=1, source_target_pairs={{0,480},{32,0},{64,32},{96,64},{128,96},{160,128},{192,160},{224,1... | collective-permute-start | bytes 786440 | tf_op jit(solution)/shard_map/ppermute | solution.py:21
  139.1 7.0 %collective-permute-start.14 = (bf16[32,4096]{1,0:T(8,128)(2,1)S(1)}, bf16[32,4096]{1,0:T(8,128)(2,1)S(1)}, u32[]{:S(2)}, u32[]{:S(2)}) collective-permute-start(bf16[32,4096]{1,0:T(8,128)(2,1)S(1)} %collective-permute-done.12), channel_id=1, source_target_pairs={{0,32},{32,64},{64,96},{96,128},{128,160},{160,192},{192,224},{224... | collective-permute-start | bytes 786440 | tf_op jit(solution)/shard_map/ppermute | solution.py:18
